TPU v7x, 32 devices: a whole 2x2x4 slice. The times are simulated.
32 devices in a mesh: cols: 8 (over z, y), chan: 4 (over x, core).
Axes of the slice: x: 2, y: 2, z: 4, core: 2. Of those that a mesh axis runs over, the one named last changes fastest.
Arguments:
- anomaly: bfloat16 [2048, 80, 128], P('cols'), may hold values from -6 to 6
- jacobian: bfloat16 [1024, 256, 128], P(('cols', 'chan')), may hold values from -0.5 to 0.5
- foot_cols: int32 [1024, 4], P('cols'), may hold values from 0 to 2047, as said below
- foot_weight: float32 [1024, 4], P('cols'), may hold values from 0.1 to 1
- obs_count: int32 [8], P('cols'), may hold values from 32 to 128, as said below
- obs_weight: bfloat16 [256, 1024], P(None, ('cols', 'chan')), may hold values from 0.25 to 4
Outputs:
- radiance_pert: bfloat16 [80, 256, 1024], P(None, 'chan', 'cols')
- ensemble_gram: float32 [64, 80, 80], P('cols', 'chan')
Inputs may be any that keep to these rules, and one draw needn't show every extreme that they name: `foot_cols`: the footprint columns of an observation of tile t lie among the columns t * 256 - 32 to (t + 1) * 256 + 31, taken modulo 2048. The live observations of tile t are its first obs_count[t] slots; in every draw at least one tile has all 128 slots live.
All inputs are finite; a program needn't handle non-finite values.
Results may differ from a plain program's by a relative error of at most 0.0095.
Values may be sent and summed in bfloat16 or wider, within the bound.
A program may use at most 64 MiB of HBM per device.

v0:
```python
import jax
import jax.numpy as jnp
from jax import lax
from jax.sharding import PartitionSpec as P

CH = 256
OBS_DEV = 128
HALO = 32
PTS = 8


def extended_2(block, sides, width):
    for axis, dim in sides:
        count = lax.axis_size(axis)
        forward = [(i, i + 1) for i in range(count - 1)]
        forward.append((count - 1, 0))
        backward = [(target, source) for source, target in forward]
        low = lax.ppermute(
            lax.slice_in_dim(block, block.shape[dim] - width, None, axis=dim), axis, forward
        )
        high = lax.ppermute(lax.slice_in_dim(block, 0, width, axis=dim), axis, backward)
        block = jnp.concatenate([low, block, high], axis=dim)
    return block


def taper(distance, half_width):
    relative = jnp.abs(distance) / half_width
    near_part = (
        ((-0.25 * relative + 0.5) * relative + 0.625) * relative - 5.0 / 3.0
    ) * relative * relative + 1.0
    bounded = jnp.maximum(relative, 1.0)
    far_part = (
        ((((relative / 12.0 - 0.5) * relative + 0.625) * relative + 5.0 / 3.0) * relative - 5.0)
        * relative
        + 4.0
        - 2.0 / (3.0 * bounded)
    )
    return jnp.where(relative <= 1.0, near_part, jnp.where(relative <= 2.0, far_part, 0.0))


def local_gram(perturbed, error_weight, centers, tile_cols):
    spacing = tile_cols / PTS
    points = (jnp.arange(PTS, dtype=jnp.float32) + 0.5) * spacing
    locality = taper(centers[None, :] - points[:, None], spacing)
    weighted = perturbed.astype(jnp.float32) * error_weight.astype(jnp.float32)
    flat_values = perturbed.reshape(perturbed.shape[0], -1)
    gram_list = []
    for point_index in range(PTS):
        scaled = (weighted * locality[point_index][None, None, :]).astype(jnp.bfloat16)
        flat_scaled = scaled.reshape(perturbed.shape[0], -1)
        gram_list.append(
            jnp.einsum("mx,kx->mk", flat_scaled, flat_values, preferred_element_type=jnp.float32)
        )
    return jnp.stack(gram_list) / (CH * OBS_DEV)


def shards(anomaly, jacobian, foot_cols, foot_weight, obs_count, obs_weight):
    col_groups = lax.axis_size("cols")
    tile_index = lax.axis_index("cols")
    chan_index = lax.axis_index("chan")
    tile_cols = anomaly.shape[0]
    obs_share = jacobian.shape[0]
    extended = extended_2(anomaly, (("cols", 0),), HALO)
    offsets = jnp.mod(foot_cols - tile_index * tile_cols + HALO, tile_cols * col_groups)
    centers = jnp.sum(foot_weight * (offsets - HALO).astype(jnp.float32), axis=1) / jnp.sum(
        foot_weight, axis=1
    )
    first_obs = chan_index * obs_share
    own_offsets = lax.dynamic_slice_in_dim(offsets, first_obs, obs_share, 0)
    own_gains = lax.dynamic_slice_in_dim(foot_weight, first_obs, obs_share, 0)
    mixed_cols = jnp.zeros((obs_share, anomaly.shape[1], anomaly.shape[2]), jnp.float32)
    for column_slot in range(own_offsets.shape[1]):
        mixed_cols = mixed_cols + own_gains[:, column_slot, None, None] * extended[
            own_offsets[:, column_slot]
        ].astype(jnp.float32)
    mixed_cols = mixed_cols.astype(jnp.bfloat16)
    radiance = jnp.einsum("ncl,nml->mcn", jacobian, mixed_cols, preferred_element_type=jnp.float32)
    slot_numbers = first_obs + jnp.arange(obs_share, dtype=jnp.int32)
    live_mask = (slot_numbers < obs_count[0]).astype(jnp.float32)
    perturbed = (radiance * live_mask[None, None, :]).astype(jnp.bfloat16)
    error_weight = obs_weight[None]
    own_centers = lax.dynamic_slice_in_dim(centers, first_obs, obs_share, 0)
    partial_gram = local_gram(perturbed, error_weight, own_centers, tile_cols)
    received = lax.all_to_all(perturbed, "chan", split_axis=1, concat_axis=2, tiled=True)
    gram_rows = lax.psum_scatter(
        partial_gram.astype(jnp.bfloat16), "chan", scatter_dimension=1, tiled=True
    ).astype(jnp.float32)
    return (received, gram_rows)


def solution(mesh):
    return jax.shard_map(
        shards,
        mesh=mesh,
        in_specs=(
            P("cols", None, None),
            P(("cols", "chan"), None, None),
            P("cols", None),
            P("cols", None),
            P("cols"),
            P(None, ("cols", "chan")),
        ),
        out_specs=(P(None, "chan", "cols"), P("cols", "chan", None)),
        check_vma=False,
    )
```

profile of v0, /device:TPU:0, one launch (start us, length us, event | category | flops | bytes accessed | tf_op | source)
XLA Modules:
  0.0 120.4 jit_solution(7480939596906263955)
XLA Ops:
  7.2 1.5 %fusion.54 = (bf16[32,80,128]{2,1,0:T(8,128)(2,1)S(1)}, bf16[32,80,128]{2,1,0:T(8,128)(2,1)S(1)}) fusion(bf16[256,80,128]{2,1,0:T(8,128)(2,1)} %param.6), kind=kLoop, calls=%fused_computation.105 | loop fusion | bytes 2621440 | tf_op jit(solution)/shard_map/slice | solution.py:21
  8.7 3.0 %collective-permute-start = (bf16[32,80,128]{2,1,0:T(8,128)(2,1)S(1)}, bf16[32,80,128]{2,1,0:T(8,128)(2,1)}, u32[]{:S(2)}, u32[]{:S(2)}) collective-permute-start(bf16[32,80,128]{2,1,0:T(8,128)(2,1)S(1)} %get-tuple-element.12), channel_id=1, source_target_pairs={{0,4},{4,8},{8,12},{12,16},{16,20},{20,24},{24,28},{28,0},{1,5},{5... | collective-permute-start | bytes 1966088 | tf_op jit(solution)/shard_map/ppermute | solution.py:18
  11.8 3.1 %collective-permute-start.1 = (bf16[32,80,128]{2,1,0:T(8,128)(2,1)S(1)}, bf16[32,80,128]{2,1,0:T(8,128)(2,1)}, u32[]{:S(2)}, u32[]{:S(2)}) collective-permute-start(bf16[32,80,128]{2,1,0:T(8,128)(2,1)S(1)} %get-tuple-element.11), channel_id=1, source_target_pairs={{4,0},{8,4},{12,8},{16,12},{20,16},{24,20},{28,24},{0,28},{5,1},{9... | collective-permute-start | bytes 1966088 | tf_op jit(solution)/shard_map/ppermute | solution.py:21
  15.5 0.1 constant_dynamic-slice_fusion.1
  15.7 0.1 constant_dynamic-slice_fusion
  15.8 0.1 dynamic_slice.11
  15.9 0.1 fusion.46
  16.0 23.8 %collective-permute-done = bf16[32,80,128]{2,1,0:T(8,128)(2,1)} collective-permute-done((bf16[32,80,128]{2,1,0:T(8,128)(2,1)S(1)}, bf16[32,80,128]{2,1,0:T(8,128)(2,1)}, u32[]{:S(2)}, u32[]{:S(2)}) %collective-permute-start) | collective-permute-done | bytes 655392 | tf_op jit(solution)/shard_map/ppermute | solution.py:18
  39.8 2.0 %constant_dynamic-update-slice_fusion.2 = bf16[320,80,128]{2,1,0:T(8,128)(2,1)} fusion(bf16[32,80,128]{2,1,0:T(8,128)(2,1)} %collective-permute-done), kind=kLoop, calls=%fused_computation.63 | loop fusion | bytes 1310720
  41.8 5.7 %constant_dynamic-update-slice_fusion.1 = bf16[320,80,128]{2,1,0:T(8,128)(2,1)} fusion(bf16[320,80,128]{2,1,0:T(8,128)(2,1)} %constant_dynamic-update-slice_fusion.2, bf16[256,80,128]{2,1,0:T(8,128)(2,1)} %param.6), kind=kLoop, calls=%fused_computation.62 | loop fusion | bytes 10485760
  47.5 2.0 %constant_dynamic-update-slice_fusion = bf16[320,80,128]{2,1,0:T(8,128)(2,1)} fusion(bf16[320,80,128]{2,1,0:T(8,128)(2,1)} %constant_dynamic-update-slice_fusion.1, bf16[32,80,128]{2,1,0:T(8,128)(2,1)} %collective-permute-done.1), kind=kLoop, calls=%fused_computation.61 | loop fusion | bytes 1310720 | tf_op jit(solution)/shard_map/concatenate | solution.py:22
  49.5 4.3 %gather_fusion.3 = bf16[32,80,128]{2,1,0:T(8,128)(2,1)} fusion(bf16[320,80,128]{2,1,0:T(8,128)(2,1)} %constant_dynamic-update-slice_fusion, s32[1024]{0:T(1024)S(1)} %get-tuple-element.29), kind=kCustom, calls=%fused_computation.3 | custom fusion | bytes 1310848 | tf_op jit(solution)/shard_map/gather | solution.py:73
  53.8 4.4 %gather_fusion.2 = bf16[32,80,128]{2,1,0:T(8,128)(2,1)} fusion(bf16[320,80,128]{2,1,0:T(8,128)(2,1)} %constant_dynamic-update-slice_fusion, s32[1024]{0:T(1024)S(1)} %get-tuple-element.30), kind=kCustom, calls=%fused_computation.2 | custom fusion | bytes 1310848 | tf_op jit(solution)/shard_map/gather | solution.py:73
  58.2 4.3 %gather_fusion.1 = bf16[32,80,128]{2,1,0:T(8,128)(2,1)} fusion(bf16[320,80,128]{2,1,0:T(8,128)(2,1)} %constant_dynamic-update-slice_fusion, s32[1024]{0:T(1024)S(1)} %get-tuple-element.31), kind=kCustom, calls=%fused_computation.1 | custom fusion | bytes 1310848 | tf_op jit(solution)/shard_map/gather | solution.py:73
  62.5 4.4 %gather_fusion = bf16[32,80,128]{2,1,0:T(8,128)(2,1)} fusion(bf16[320,80,128]{2,1,0:T(8,128)(2,1)} %constant_dynamic-update-slice_fusion, s32[1024]{0:T(1024)S(1)} %get-tuple-element.32), kind=kCustom, calls=%fused_computation | custom fusion | bytes 1310848 | tf_op jit(solution)/shard_map/gather | solution.py:73
  66.9 2.6 %fusion.8 = bf16[80,256,32]{1,0,2:T(8,128)(2,1)S(1)} fusion(bf16[32,256,128]{2,1,0:T(8,128)(2,1)S(1)} %copy-done, f32[32]{0:T(128)S(1)} %compare_convert_fusion, bf16[32,80,128]{2,1,0:T(8,128)(2,1)} %gather_fusion.3, bf16[32,80,128]{2,1,0:T(8,128)(2,1)} %gather_fusion.2, bf16[32,80,128]{2,1,0:T(8,128)(2,1)} %gather_fusion.1, ...), kind=kOutput, calls=%fused_computation.22 | convolution fusion | flops 173015040 | bytes 6029952 | tf_op jit(solution)/shard_map/ncl,nml->mcn/dot_general | solution.py:77
  69.5 3.0 %copy.14 = bf16[80,256,32]{0,2,1:T(8,128)(2,1)} copy(bf16[80,256,32]{1,0,2:T(8,128)(2,1)S(1)} %fusion.8) | data formatting | bytes 2621440 | tf_op jit(solution)/shard_map/convert_element_type | solution.py:80
  72.5 4.4 %all-to-all-start = ((bf16[80,256,32]{0,2,1:T(8,128)(2,1)}), bf16[80,256,32]{0,2,1:T(8,128)(2,1)}, u32[]{:S(2)}, u32[]{:S(2)}) async-start(bf16[80,256,32]{0,2,1:T(8,128)(2,1)} %copy.14), calls=%async_computation | async-start | bytes 4194304 | tf_op jit(solution)/shard_map/all_to_all | solution.py:84
  76.9 0.0 reduce-scatter.2.cloned.1.call-start
  77.0 0.6 fusion.40
  77.6 0.6 fusion.38
  78.1 0.6 fusion.36
  78.7 0.6 fusion.34
  79.2 0.6 fusion.32
  79.8 0.6 fusion.30
  80.4 0.6 fusion.28
  80.9 0.6 fusion.26
  81.5 0.7 copy.16
  82.3 22.6 %reduce-scatter.2.cloned.1.call-done = bf16[8,20,80]{2,0,1:T(8,128)(2,1)} async-done(((bf16[8,80,80]{2,0,1:T(8,128)(2,1)}), bf16[8,20,80]{2,0,1:T(8,128)(2,1)}) %reduce-scatter.2.cloned.1.call-update) | async-done | bytes 25616 | tf_op jit(solution)/shard_map/reduce_scatter | solution.py:85
  104.9 1.4 %convert_element_type.88 = f32[8,20,80]{2,0,1:T(8,128)} convert(bf16[8,20,80]{2,0,1:T(8,128)(2,1)} %reduce-scatter.2.cloned.1.call-done) | non-fusion elementwise | flops 12800 | bytes 76800 | tf_op jit(solution)/shard_map/convert_element_type | solution.py:87
  106.3 3.6 %copy.15 = bf16[80,64,4,32]{0,3,2,1:T(8,128)(2,1)} copy(bf16[80,64,4,32]{0,3,1,2:T(8,128)(2,1)} %bitcast.11) | data formatting | bytes 2621440 | tf_op jit(solution)/shard_map/all_to_all | solution.py:84
  109.9 3.7 %copy.17 = bf16[80,64,128]{2,1,0:T(8,128)(2,1)} copy(bf16[80,64,128]{0,2,1:T(8,128)(2,1)} %bitcast.89) | data formatting | bytes 2621440
  (22 shorter events, 0.2 us)
Async XLA Ops:
  7.2 59.7 %copy-start = (bf16[32,256,128]{2,1,0:T(8,128)(2,1)S(1)}, bf16[32,256,128]{2,1,0:T(8,128)(2,1)}, u32[]{:S(2)}) copy-start(bf16[32,256,128]{2,1,0:T(8,128)(2,1)} %param.7) | copy-start | bytes 6291460
  7.2 8.4 %copy-start.2 = (f32[128,4]{0,1:T(4,128)S(1)}, f32[128,4]{0,1:T(4,128)}, u32[]{:S(2)}) copy-start(f32[128,4]{0,1:T(4,128)} %param.9) | copy-start | bytes 6148
  7.2 8.4 %copy-start.3 = (s32[128,4]{0,1:T(4,128)S(1)}, s32[128,4]{0,1:T(4,128)}, u32[]{:S(2)}) copy-start(s32[128,4]{0,1:T(4,128)} %param.8) | copy-start | bytes 6148
  7.2 8.6 %copy-start.1 = (bf16[256,32]{0,1:T(8,128)(2,1)S(1)}, bf16[256,32]{0,1:T(8,128)(2,1)}, u32[]{:S(2)}) copy-start(bf16[256,32]{0,1:T(8,128)(2,1)} %param.11) | copy-start | bytes 49156
  8.7 31.1 %collective-permute-start = (bf16[32,80,128]{2,1,0:T(8,128)(2,1)S(1)}, bf16[32,80,128]{2,1,0:T(8,128)(2,1)}, u32[]{:S(2)}, u32[]{:S(2)}) collective-permute-start(bf16[32,80,128]{2,1,0:T(8,128)(2,1)S(1)} %get-tuple-element.12), channel_id=1, source_target_pairs={{0,4},{4,8},{8,12},{12,16},{16,20},{20,24},{24,28},{28,0},{1,5},{5... | collective-permute-start | bytes 1966088 | tf_op jit(solution)/shard_map/ppermute | solution.py:18
  11.8 35.7 %collective-permute-start.1 = (bf16[32,80,128]{2,1,0:T(8,128)(2,1)S(1)}, bf16[32,80,128]{2,1,0:T(8,128)(2,1)}, u32[]{:S(2)}, u32[]{:S(2)}) collective-permute-start(bf16[32,80,128]{2,1,0:T(8,128)(2,1)S(1)} %get-tuple-element.11), channel_id=1, source_target_pairs={{4,0},{8,4},{12,8},{16,12},{20,16},{24,20},{28,24},{0,28},{5,1},{9... | collective-permute-start | bytes 1966088 | tf_op jit(solution)/shard_map/ppermute | solution.py:21
  72.5 33.8 %all-to-all-start = ((bf16[80,256,32]{0,2,1:T(8,128)(2,1)}), bf16[80,256,32]{0,2,1:T(8,128)(2,1)}, u32[]{:S(2)}, u32[]{:S(2)}) async-start(bf16[80,256,32]{0,2,1:T(8,128)(2,1)} %copy.14), calls=%async_computation | async-start | bytes 4194304 | tf_op jit(solution)/shard_map/all_to_all | solution.py:84
  76.9 27.9 %reduce-scatter.2.cloned.1.call-start = ((), (), s32[]{:S(2)}) async-start(), calls=%async_computation.2 | async-start | bytes 204800 | tf_op jit(solution)/shard_map/reduce_scatter | solution.py:85
Sparse Core Ops, SparseCore 0:
  82.4 22.4 reduce-scatter.1
where the time goes:
time: 121 us; the launch traced here: 120 us
  waiting for transfers between devices  46.5 us (38%)
  local copies, waits for them, and re-layouts  39.8 us (33%)
  between operations  14.9 us (12%)
  starting transfers between devices  10.6 us (9%)
  matrix products  7.02 us (6%)
  other arithmetic  1.61 us (1%)
    ppermute x1, waiting for transfers between devices, extended_2(): lax.ppermute(lax.slice_in_dim(block, block.shape[dim] - width, None, axis...  23.8 us
    reduce_scatter x1, waiting for transfers between devices, shards(): lax.psum_scatter(partial_gram.astype(jnp.bfloat16), 'chan', scatter_dimen...  22.6 us
    gather x4, local copies, waits for them, and re-layouts, shards(): extended[own_offsets[:, column_slot]].astype(jnp.float32)  17.4 us
    unnamed x11, local copies, waits for them, and re-layouts  11.4 us
    all_to_all x1, starting transfers between devices, shards(): lax.all_to_all(perturbed, 'chan', split_axis=1, concat_axis=2, tiled=True)  4.45 us
    dot_general x8, matrix products, local_gram(): jnp.einsum('mx,kx->mk', flat_scaled, flat_values, preferred_element_type=...  4.43 us
    all_to_all x1, local copies, waits for them, and re-layouts, shards(): lax.all_to_all(perturbed, 'chan', split_axis=1, concat_axis=2, tiled=True)  3.56 us
    ppermute x1, starting transfers between devices, extended_2(): lax.ppermute(lax.slice_in_dim(block, 0, width, axis=dim), axis, backward)  3.1 us
  transfers between devices with their start and end apart: 4, of which 2 were waited for; matrix products, arithmetic and copies ran while one was open for 12% of the time, Pallas kernels for 0%

commit v1 on v0

--- a/solution.py
+++ b/solution.py
@@ -81,7 +81,12 @@
     error_weight = obs_weight[None]
     own_centers = lax.dynamic_slice_in_dim(centers, first_obs, obs_share, 0)
     partial_gram = local_gram(perturbed, error_weight, own_centers, tile_cols)
-    received = lax.all_to_all(perturbed, "chan", split_axis=1, concat_axis=2, tiled=True)
+    received = jnp.concatenate(
+        lax.all_to_all(
+            jnp.stack(jnp.split(perturbed, lax.axis_size("chan"), axis=1)), "chan", 0, 0
+        ),
+        axis=2,
+    )
     gram_rows = lax.psum_scatter(
         partial_gram.astype(jnp.bfloat16), "chan", scatter_dimension=1, tiled=True
     ).astype(jnp.float32)

time: 121 us -> 126 us (1.041)
  local copies, waits for them, and re-layouts: 39.8 us -> 42.8 us
  other arithmetic: 1.61 us -> 3.81 us
    another operation x0 -> x2, local copies, waits for them, and re-layouts: none -> 5.94 us  [shards(): jnp.stack(jnp.split(perturbed, lax.axis_size('chan'), axis=1))]
    reshape x0 -> x1, local copies, waits for them, and re-layouts: none -> 3.57 us  [shards(): jnp.concatenate(lax.all_to_all(jnp.stack(jnp.split(perturbed, lax.axis_si...]
    all_to_all x1 -> x0, local copies, waits for them, and re-layouts: 3.56 us -> none  [shards(): lax.all_to_all(perturbed, 'chan', split_axis=1, concat_axis=2, tiled=True)]
    convert_element_type x1 -> x0, local copies, waits for them, and re-layouts: 3.02 us -> none  [shards(): perturbed = (radiance * live_mask[None, None, :]).astype(jnp.bfloat16)]
    another operation x0 -> x1, other arithmetic: none -> 2.2 us  [shards(): jnp.stack(jnp.split(perturbed, lax.axis_size('chan'), axis=1))]
where the time goes in v1:
time: 126 us
  waiting for transfers between devices  46.5 us (37%)
  local copies, waits for them, and re-layouts  42.8 us (34%)
  between operations  14.9 us (12%)
  starting transfers between devices  10.6 us (8%)
  matrix products  7.01 us (6%)
  other arithmetic  3.81 us (3%)
    ppermute x1, waiting for transfers between devices, extended_2(): lax.ppermute(lax.slice_in_dim(block, block.shape[dim] - width, None, axis...  23.8 us
    reduce_scatter x1, waiting for transfers between devices, shards(): lax.psum_scatter(partial_gram.astype(jnp.bfloat16), 'chan', scatter_dimen...  22.6 us
    gather x4, local copies, waits for them, and re-layouts, shards(): extended[own_offsets[:, column_slot]].astype(jnp.float32)  17.4 us
    unnamed x11, local copies, waits for them, and re-layouts  11.4 us
    another operation x2, local copies, waits for them, and re-layouts, shards(): jnp.stack(jnp.split(perturbed, lax.axis_size('chan'), axis=1))  5.94 us
    all_to_all x1, starting transfers between devices, shards(): lax.all_to_all(jnp.stack(jnp.split(perturbed, lax.axis_size('chan'), axis...  4.44 us
    dot_general x8, matrix products, local_gram(): jnp.einsum('mx,kx->mk', flat_scaled, flat_values, preferred_element_type=...  4.42 us
    reshape x1, local copies, waits for them, and re-layouts, shards(): jnp.concatenate(lax.all_to_all(jnp.stack(jnp.split(perturbed, lax.axis_si...  3.57 us
  transfers between devices with their start and end apart: 4, of which 2 were waited for; matrix products, arithmetic and copies ran while one was open for 12% of the time, Pallas kernels for 0%

profile of v1, /device:TPU:0, one launch (start us, length us, event | category | flops | bytes accessed | tf_op | source)
XLA Modules:
  0.0 125.6 jit_solution(4361788523839178280)
XLA Ops:
  7.2 1.5 %fusion.54 = (bf16[32,80,128]{2,1,0:T(8,128)(2,1)S(1)}, bf16[32,80,128]{2,1,0:T(8,128)(2,1)S(1)}) fusion(bf16[256,80,128]{2,1,0:T(8,128)(2,1)} %param.6), kind=kLoop, calls=%fused_computation.110 | loop fusion | bytes 2621440 | tf_op jit(solution)/shard_map/slice | solution.py:21
  8.7 3.0 %collective-permute-start = (bf16[32,80,128]{2,1,0:T(8,128)(2,1)S(1)}, bf16[32,80,128]{2,1,0:T(8,128)(2,1)}, u32[]{:S(2)}, u32[]{:S(2)}) collective-permute-start(bf16[32,80,128]{2,1,0:T(8,128)(2,1)S(1)} %get-tuple-element.10), channel_id=1, source_target_pairs={{0,4},{4,8},{8,12},{12,16},{16,20},{20,24},{24,28},{28,0},{1,5},{5... | collective-permute-start | bytes 1966088 | tf_op jit(solution)/shard_map/ppermute | solution.py:18
  11.8 3.1 %collective-permute-start.1 = (bf16[32,80,128]{2,1,0:T(8,128)(2,1)S(1)}, bf16[32,80,128]{2,1,0:T(8,128)(2,1)}, u32[]{:S(2)}, u32[]{:S(2)}) collective-permute-start(bf16[32,80,128]{2,1,0:T(8,128)(2,1)S(1)} %get-tuple-element.9), channel_id=1, source_target_pairs={{4,0},{8,4},{12,8},{16,12},{20,16},{24,20},{28,24},{0,28},{5,1},{9... | collective-permute-start | bytes 1966088 | tf_op jit(solution)/shard_map/ppermute | solution.py:21
  15.5 0.1 constant_dynamic-slice_fusion.1
  15.8 0.1 dynamic_slice.11
  15.9 0.1 fusion.46
  16.0 23.8 %collective-permute-done = bf16[32,80,128]{2,1,0:T(8,128)(2,1)} collective-permute-done((bf16[32,80,128]{2,1,0:T(8,128)(2,1)S(1)}, bf16[32,80,128]{2,1,0:T(8,128)(2,1)}, u32[]{:S(2)}, u32[]{:S(2)}) %collective-permute-start) | collective-permute-done | bytes 655392 | tf_op jit(solution)/shard_map/ppermute | solution.py:18
  39.8 2.0 %constant_dynamic-update-slice_fusion.2 = bf16[320,80,128]{2,1,0:T(8,128)(2,1)} fusion(bf16[32,80,128]{2,1,0:T(8,128)(2,1)} %collective-permute-done), kind=kLoop, calls=%fused_computation.68 | loop fusion | bytes 1310720
  41.8 5.7 %constant_dynamic-update-slice_fusion.1 = bf16[320,80,128]{2,1,0:T(8,128)(2,1)} fusion(bf16[320,80,128]{2,1,0:T(8,128)(2,1)} %constant_dynamic-update-slice_fusion.2, bf16[256,80,128]{2,1,0:T(8,128)(2,1)} %param.6), kind=kLoop, calls=%fused_computation.67 | loop fusion | bytes 10485760
  47.5 2.0 %constant_dynamic-update-slice_fusion = bf16[320,80,128]{2,1,0:T(8,128)(2,1)} fusion(bf16[320,80,128]{2,1,0:T(8,128)(2,1)} %constant_dynamic-update-slice_fusion.1, bf16[32,80,128]{2,1,0:T(8,128)(2,1)} %collective-permute-done.1), kind=kLoop, calls=%fused_computation.66 | loop fusion | bytes 1310720 | tf_op jit(solution)/shard_map/concatenate | solution.py:22
  49.5 4.3 %gather_fusion.3 = bf16[32,80,128]{2,1,0:T(8,128)(2,1)} fusion(bf16[320,80,128]{2,1,0:T(8,128)(2,1)} %constant_dynamic-update-slice_fusion, s32[1024]{0:T(1024)S(1)} %get-tuple-element.31), kind=kCustom, calls=%fused_computation.3 | custom fusion | bytes 1310848 | tf_op jit(solution)/shard_map/gather | solution.py:73
  53.8 4.3 %gather_fusion.2 = bf16[32,80,128]{2,1,0:T(8,128)(2,1)} fusion(bf16[320,80,128]{2,1,0:T(8,128)(2,1)} %constant_dynamic-update-slice_fusion, s32[1024]{0:T(1024)S(1)} %get-tuple-element.32), kind=kCustom, calls=%fused_computation.2 | custom fusion | bytes 1310848 | tf_op jit(solution)/shard_map/gather | solution.py:73
  58.2 4.3 %gather_fusion.1 = bf16[32,80,128]{2,1,0:T(8,128)(2,1)} fusion(bf16[320,80,128]{2,1,0:T(8,128)(2,1)} %constant_dynamic-update-slice_fusion, s32[1024]{0:T(1024)S(1)} %get-tuple-element.33), kind=kCustom, calls=%fused_computation.1 | custom fusion | bytes 1310848 | tf_op jit(solution)/shard_map/gather | solution.py:73
  62.5 4.4 %gather_fusion = bf16[32,80,128]{2,1,0:T(8,128)(2,1)} fusion(bf16[320,80,128]{2,1,0:T(8,128)(2,1)} %constant_dynamic-update-slice_fusion, s32[1024]{0:T(1024)S(1)} %get-tuple-element.34), kind=kCustom, calls=%fused_computation | custom fusion | bytes 1310848 | tf_op jit(solution)/shard_map/gather | solution.py:73
  66.9 2.6 %fusion.8 = bf16[80,256,32]{1,0,2:T(8,128)(2,1)S(1)} fusion(bf16[32,256,128]{2,1,0:T(8,128)(2,1)S(1)} %copy-done, f32[32]{0:T(128)S(1)} %compare_convert_fusion, bf16[32,80,128]{2,1,0:T(8,128)(2,1)} %gather_fusion.3, bf16[32,80,128]{2,1,0:T(8,128)(2,1)} %gather_fusion.2, bf16[32,80,128]{2,1,0:T(8,128)(2,1)} %gather_fusion.1, ...), kind=kOutput, calls=%fused_computation.23 | convolution fusion | flops 173015040 | bytes 6029952 | tf_op jit(solution)/shard_map/ncl,nml->mcn/dot_general | solution.py:77
  69.5 0.6 slice_bitcast_fusion.3
  70.1 2.2 %pad_maximum_fusion = bf16[4,80,64,32]{2,1,3,0:T(8,128)(2,1)} fusion(bf16[1,80,64,32]{2,1,3,0:T(8,128)(2,1)S(1)} %get-tuple-element.12, bf16[1,80,64,32]{2,1,3,0:T(8,128)(2,1)S(1)} %get-tuple-element.13, bf16[1,80,64,32]{2,1,3,0:T(8,128)(2,1)S(1)} %get-tuple-element.14, bf16[1,80,64,32]{2,1,3,0:T(8,128)(2,1)S(1)} %get-tuple-element.11), kind=kLoop, calls=%fused_computation.4 | loop fusion | flops 1966080 | bytes 2621440 | tf_op jit(solution)/shard_map/stack | solution.py:86
  72.3 5.3 %copy.12 = bf16[4,80,64,32]{1,3,2,0:T(8,128)(2,1)} copy(bf16[4,80,64,32]{2,1,3,0:T(8,128)(2,1)} %pad_maximum_fusion) | data formatting | bytes 2621440 | tf_op jit(solution)/shard_map/stack | solution.py:86
  77.6 4.4 %all-to-all-start = ((bf16[4,80,64,32]{1,3,2,0:T(8,128)(2,1)}), bf16[4,80,64,32]{1,3,2,0:T(8,128)(2,1)}, u32[]{:S(2)}, u32[]{:S(2)}) async-start(bf16[4,80,64,32]{1,3,2,0:T(8,128)(2,1)} %copy.12), calls=%async_computation | async-start | bytes 4194304 | tf_op jit(solution)/shard_map/all_to_all | solution.py:85
  82.1 0.6 fusion.40
  82.7 0.6 fusion.38
  83.2 0.6 fusion.36
  83.8 0.5 fusion.34
  84.4 0.6 fusion.32
  84.9 0.6 fusion.30
  85.5 0.6 fusion.28
  86.0 0.6 fusion.26
  86.6 0.7 copy.14
  87.4 22.6 %reduce-scatter.2.cloned.1.call-done = bf16[8,20,80]{2,0,1:T(8,128)(2,1)} async-done(((bf16[8,80,80]{2,0,1:T(8,128)(2,1)}), bf16[8,20,80]{2,0,1:T(8,128)(2,1)}) %reduce-scatter.2.cloned.1.call-update) | async-done | bytes 25616 | tf_op jit(solution)/shard_map/reduce_scatter | solution.py:90
  110.0 1.4 %convert_element_type.88 = f32[8,20,80]{2,0,1:T(8,128)} convert(bf16[8,20,80]{2,0,1:T(8,128)(2,1)} %reduce-scatter.2.cloned.1.call-done) | non-fusion elementwise | flops 12800 | bytes 76800 | tf_op jit(solution)/shard_map/convert_element_type | solution.py:92
  111.4 3.6 %copy.13 = bf16[80,64,4,32]{0,3,2,1:T(8,128)(2,1)} copy(bf16[80,64,4,32]{0,3,1,2:T(8,128)(2,1)} %bitcast.14) | data formatting | bytes 2621440 | tf_op jit(solution)/shard_map/reshape | solution.py:84
  115.0 3.7 %copy.15 = bf16[80,64,128]{2,1,0:T(8,128)(2,1)} copy(bf16[80,64,128]{0,2,1:T(8,128)(2,1)} %bitcast.95) | data formatting | bytes 2621440
  (24 shorter events, 0.3 us)
Async XLA Ops:
  7.2 59.7 %copy-start = (bf16[32,256,128]{2,1,0:T(8,128)(2,1)S(1)}, bf16[32,256,128]{2,1,0:T(8,128)(2,1)}, u32[]{:S(2)}) copy-start(bf16[32,256,128]{2,1,0:T(8,128)(2,1)} %param.7) | copy-start | bytes 6291460
  7.2 8.4 %copy-start.2 = (f32[128,4]{0,1:T(4,128)S(1)}, f32[128,4]{0,1:T(4,128)}, u32[]{:S(2)}) copy-start(f32[128,4]{0,1:T(4,128)} %param.9) | copy-start | bytes 6148
  7.2 8.4 %copy-start.3 = (s32[128,4]{0,1:T(4,128)S(1)}, s32[128,4]{0,1:T(4,128)}, u32[]{:S(2)}) copy-start(s32[128,4]{0,1:T(4,128)} %param.8) | copy-start | bytes 6148
  7.2 8.6 %copy-start.1 = (bf16[256,32]{0,1:T(8,128)(2,1)S(1)}, bf16[256,32]{0,1:T(8,128)(2,1)}, u32[]{:S(2)}) copy-start(bf16[256,32]{0,1:T(8,128)(2,1)} %param.11) | copy-start | bytes 49156
  8.7 31.1 %collective-permute-start = (bf16[32,80,128]{2,1,0:T(8,128)(2,1)S(1)}, bf16[32,80,128]{2,1,0:T(8,128)(2,1)}, u32[]{:S(2)}, u32[]{:S(2)}) collective-permute-start(bf16[32,80,128]{2,1,0:T(8,128)(2,1)S(1)} %get-tuple-element.10), channel_id=1, source_target_pairs={{0,4},{4,8},{8,12},{12,16},{16,20},{20,24},{24,28},{28,0},{1,5},{5... | collective-permute-start | bytes 1966088 | tf_op jit(solution)/shard_map/ppermute | solution.py:18
  11.8 35.7 %collective-permute-start.1 = (bf16[32,80,128]{2,1,0:T(8,128)(2,1)S(1)}, bf16[32,80,128]{2,1,0:T(8,128)(2,1)}, u32[]{:S(2)}, u32[]{:S(2)}) collective-permute-start(bf16[32,80,128]{2,1,0:T(8,128)(2,1)S(1)} %get-tuple-element.9), channel_id=1, source_target_pairs={{4,0},{8,4},{12,8},{16,12},{20,16},{24,20},{28,24},{0,28},{5,1},{9... | collective-permute-start | bytes 1966088 | tf_op jit(solution)/shard_map/ppermute | solution.py:21
  77.6 33.8 %all-to-all-start = ((bf16[4,80,64,32]{1,3,2,0:T(8,128)(2,1)}), bf16[4,80,64,32]{1,3,2,0:T(8,128)(2,1)}, u32[]{:S(2)}, u32[]{:S(2)}) async-start(bf16[4,80,64,32]{1,3,2,0:T(8,128)(2,1)} %copy.12), calls=%async_computation | async-start | bytes 4194304 | tf_op jit(solution)/shard_map/all_to_all | solution.py:85
  82.1 27.9 %reduce-scatter.2.cloned.1.call-start = ((), (), s32[]{:S(2)}) async-start(), calls=%async_computation.2 | async-start | bytes 204800 | tf_op jit(solution)/shard_map/reduce_scatter | solution.py:90
Sparse Core Ops, SparseCore 0:
  87.5 22.4 reduce-scatter.1
